TPU v7x, 512 devices: a whole 4x4x16 slice. The times are simulated.
512 devices in a mesh: row: 32 (over z, y_lo), col: 16 (over y_hi, x, core).
Axes of the slice: x: 4, y: 4 (y_hi: 2, y_lo: 2; y = y_hi * 2 + y_lo), z: 16, core: 2. Of those that a mesh axis runs over, the one named last changes fastest.
Arguments:
- coords: int32 [3, 65536], P(None, ('row', 'col')), may hold values from 0 to 60809, as said below
- mode_shapes: bfloat16 [256, 65536], P(None, ('row', 'col')), as said below
- output_shapes: bfloat16 [1048576, 256], P(('row', 'col')), may hold values from -0.375 to 0.375
- response_gain: float32 [2, 256], replicated, may hold values from -4 to 4
Outputs:
- response_power: float32 [1048576], P(('row', 'col'))
- modal_csd: float32 [256, 256], replicated
Inputs may be any that keep to these rules, and one draw needn't show every extreme that they name: `coords`: positions of points on an aircraft's skin, numbered in no spatial order. `mode_shapes`: entries are of order 1 / sqrt(65536); each mode has a share of one sign over all nodes.
All inputs are finite; a program needn't handle non-finite values.
Results may differ from a plain program's by a relative error of at most 0.002.
Values may be sent and summed in bfloat16 or wider, within the bound.
A program may use at most 64 MiB of HBM per device.

v0:
```python
import math
import jax
import jax.numpy as jnp
from jax import lax
from jax.sharding import PartitionSpec as P

wave_scale = 0.35 / 64.0


def coherence(left_points, right_points):
    difference = (left_points[:, :, None] - right_points[:, None, :]).astype(jnp.float32)
    squared = jnp.sum(difference * difference, axis=0)
    return jnp.sinc(wave_scale * jnp.sqrt(squared)).astype(jnp.bfloat16)


def split_parts(matrix):
    high_part = matrix.astype(jnp.bfloat16)
    low_part = (matrix - high_part.astype(jnp.float32)).astype(jnp.bfloat16)
    return (high_part, low_part)


def modal_product(node_shapes, node_projection):
    high_part, low_part = split_parts(node_projection)
    dims = (((1,), (1,)), ((), ()))
    upper = lax.dot_general(node_shapes, high_part, dims, preferred_element_type=jnp.float32)
    lower = lax.dot_general(node_shapes, low_part, dims, preferred_element_type=jnp.float32)
    return upper + lower


def local(coords, mode_shapes, output_shapes, response_gain):
    row_shapes, row_points = (
        lax.all_gather(mode_shapes, "col", axis=1, tiled=True),
        lax.all_gather(coords, "col", axis=1, tiled=True),
    )
    mode_count = mode_shapes.shape[0]
    zero_block = jnp.zeros((mode_count, row_points.shape[1]), jnp.float32)
    piece_shapes = lax.all_gather(mode_shapes, "row", axis=1, tiled=True)
    piece_points = lax.all_gather(coords, "row", axis=1, tiled=True)
    length = piece_shapes.shape[1]
    block_size = math.gcd(length, 1024)
    block_count = length // block_size

    def add_block(loop_index, running_sum):
        block_start = loop_index * block_size
        part_shapes = lax.dynamic_slice_in_dim(piece_shapes, block_start, block_size, 1)
        part_points = lax.dynamic_slice_in_dim(piece_points, block_start, block_size, 1)
        coherence_tile = coherence(part_points, row_points)
        return running_sum + jnp.dot(
            part_shapes, coherence_tile, preferred_element_type=jnp.float32
        )

    projection = lax.fori_loop(0, block_count, add_block, zero_block)
    partial_csd = modal_product(row_shapes, projection)
    modal_csd = lax.psum(partial_csd, ("row", "col"))
    real_part = response_gain[0]
    imag_part = response_gain[1]
    weighted = (
        real_part[:, None] * real_part[None, :] + imag_part[:, None] * imag_part[None, :]
    ) * modal_csd
    weighted_high, weighted_low = split_parts(weighted)
    mapped = jnp.dot(output_shapes, weighted_high, preferred_element_type=jnp.float32)
    mapped = mapped + jnp.dot(output_shapes, weighted_low, preferred_element_type=jnp.float32)
    response_power = jnp.sum(mapped * output_shapes.astype(jnp.float32), axis=1)
    return (response_power, modal_csd)


def solution(mesh):
    in_specs = (P(None, ("row", "col")), P(None, ("row", "col")), P(("row", "col"), None), P())
    out_specs = (P(("row", "col")), P())
    return jax.shard_map(local, mesh=mesh, in_specs=in_specs, out_specs=out_specs, check_vma=False)
```

profile of v0, /device:TPU:4, one launch (start us, length us, event | category | flops | bytes accessed | tf_op | source)
XLA Modules:
  0.0 702.3 jit_solution(17819532380165018910)
XLA Ops:
  7.2 0.0 all-gather.3.cloned.1.call-start
  7.2 0.7 all-gather.3.cloned.1.call-update
  7.9 0.0 all-gather.5.cloned.1.call-start
  7.9 0.7 all-gather.5.cloned.1.call-update
  8.6 0.0 all-reduce.2.cloned.1.call-start
  8.7 69.6 %all_gather.13 = s32[3,4096]{1,0:T(4,128)S(1)} all-gather(s32[3,128]{1,0:T(4,128)} %param.6), channel_id=1, replica_groups=mesh['row'=32,'col'=16] {'row'}, dimensions={1}, use_global_device_ids=true | all-gather | bytes 50688 | tf_op jit(solution)/shard_map/all_gather | solution.py:38
  78.3 19.8 %all_gather.14 = s32[3,2048]{1,0:T(4,128)S(1)} all-gather(s32[3,128]{1,0:T(4,128)} %param.6), channel_id=1, replica_groups=mesh['row'=32,'col'=16] {'col'}, dimensions={1}, use_global_device_ids=true | all-gather | bytes 26112 | tf_op jit(solution)/shard_map/all_gather | solution.py:33
  98.1 2.3 copy.8
  100.4 50.3 %all-gather.3.cloned.1.call-done = bf16[256,4096]{1,0:T(8,128)(2,1)} async-done(((bf16[256,128]{1,0:T(8,128)(2,1)}), bf16[256,4096]{1,0:T(8,128)(2,1)}) %all-gather.3.cloned.1.call-update) | async-done | bytes 2097168 | tf_op jit(solution)/shard_map/all_gather | solution.py:37
  150.7 0.0 copy-start.1
  150.7 81.9 %while.16 = (s32[]{:T(128)}, f32[256,2048]{1,0:T(8,128)S(1)}, bf16[256,4096]{1,0:T(8,128)(2,1)}, s32[3,4096]{1,0:T(4,128)S(1)}, s32[3,2048]{1,0:T(4,128)S(1)}, /*index=5*/s32[]{:T(128)}, s32[]{:T(128)}, s32[]{:T(128)}, s32[]{:T(128)}) while((s32[]{:T(128)}, f32[256,2048]{1,0:T(8,128)S(1)}, bf16[256,4096]{1,0:T(8,128)(2,1)}, ...), condition=%wide.region_2.3_spmd.clone, body=%wide.region_0.2_spmd.clone.sunk | while | flops 1171259392 | bytes 21557404 | solution.py:52
  150.7 6.3 multiply_reduce_fusion.2
  157.0 14.1 %fusion.60 = f32[256,2048]{1,0:T(8,128)S(1)} fusion(f32[1024,2048]{1,0:T(8,128)} %multiply_reduce_fusion.2, f32[256,2048]{1,0:T(8,128)S(1)} %get-tuple-element.211, pred[]{:T(512)S(6)} %compare.3, bf16[256,4096]{1,0:T(8,128)(2,1)} %get-tuple-element.221, s32[]{:T(128)S(6)} %select_n.137), kind=kOutput, calls=%fused_computation.26.clone.1 | convolution fusion | flops 1148190720 | bytes 13107205 | tf_op jit(solution)/shard_map/while/body/eval_jaxpr/dot_general | solution.py:48
  171.2 6.3 multiply_reduce_fusion.2
  177.5 14.1 %fusion.60 = f32[256,2048]{1,0:T(8,128)S(1)} fusion(f32[1024,2048]{1,0:T(8,128)} %multiply_reduce_fusion.2, f32[256,2048]{1,0:T(8,128)S(1)} %get-tuple-element.211, pred[]{:T(512)S(6)} %compare.3, bf16[256,4096]{1,0:T(8,128)(2,1)} %get-tuple-element.221, s32[]{:T(128)S(6)} %select_n.137), kind=kOutput, calls=%fused_computation.26.clone.1 | convolution fusion | flops 1148190720 | bytes 13107205 | tf_op jit(solution)/shard_map/while/body/eval_jaxpr/dot_general | solution.py:48
  191.7 6.3 multiply_reduce_fusion.2
  198.0 14.1 %fusion.60 = f32[256,2048]{1,0:T(8,128)S(1)} fusion(f32[1024,2048]{1,0:T(8,128)} %multiply_reduce_fusion.2, f32[256,2048]{1,0:T(8,128)S(1)} %get-tuple-element.211, pred[]{:T(512)S(6)} %compare.3, bf16[256,4096]{1,0:T(8,128)(2,1)} %get-tuple-element.221, s32[]{:T(128)S(6)} %select_n.137), kind=kOutput, calls=%fused_computation.26.clone.1 | convolution fusion | flops 1148190720 | bytes 13107205 | tf_op jit(solution)/shard_map/while/body/eval_jaxpr/dot_general | solution.py:48
  212.1 6.3 multiply_reduce_fusion.2
  218.5 14.1 %fusion.60 = f32[256,2048]{1,0:T(8,128)S(1)} fusion(f32[1024,2048]{1,0:T(8,128)} %multiply_reduce_fusion.2, f32[256,2048]{1,0:T(8,128)S(1)} %get-tuple-element.211, pred[]{:T(512)S(6)} %compare.3, bf16[256,4096]{1,0:T(8,128)(2,1)} %get-tuple-element.221, s32[]{:T(128)S(6)} %select_n.137), kind=kOutput, calls=%fused_computation.26.clone.1 | convolution fusion | flops 1148190720 | bytes 13107205 | tf_op jit(solution)/shard_map/while/body/eval_jaxpr/dot_general | solution.py:48
  232.6 0.0 copy-start
  232.6 0.0 all-gather.5.cloned.1.call-done
  232.6 1.8 fusion.37
  234.4 2.4 fusion.35
  236.8 0.0 all-reduce.2.cloned.1.call-update
  236.9 0.0 copy-done.1
  236.9 453.2 %all-reduce.2.cloned.1.call-done = f32[256,256]{0,1:T(8,128)} async-done(((f32[256,256]{0,1:T(8,128)}), f32[256,256]{0,1:T(8,128)}) %all-reduce.2.cloned.1.call-update) | async-done | bytes 262160 | tf_op jit(solution)/shard_map/psum | solution.py:54
  690.1 1.8 copy.9
  691.9 0.0 copy-done
  691.9 1.4 fusion.40
  693.3 2.5 fusion.34
  (6 shorter events, 0.0 us)
Async XLA Ops:
  7.2 143.5 %all-gather.3.cloned.1.call-start = ((), (), s32[]{:S(2)}) async-start(), calls=%async_computation | async-start | bytes 2162688 | tf_op jit(solution)/shard_map/all_gather | solution.py:37
  7.9 224.7 %all-gather.5.cloned.1.call-start = ((), (), s32[]{:S(2)}) async-start(), calls=%async_computation.1 | async-start | bytes 1114112 | tf_op jit(solution)/shard_map/all_gather | solution.py:32
  8.6 681.4 %all-reduce.2.cloned.1.call-start = ((), (), s32[]{:S(2)}) async-start(), calls=%async_computation.2 | async-start | bytes 524288 | tf_op jit(solution)/shard_map/psum | solution.py:54
  150.7 86.2 %copy-start.1 = (f32[2,256]{1,0:T(2,128)S(1)}, f32[2,256]{1,0:T(2,128)}, u32[]{:S(2)}) copy-start(f32[2,256]{1,0:T(2,128)} %param.9) | copy-start | bytes 6148
  232.6 459.3 %copy-start = (bf16[2048,256]{1,0:T(8,128)(2,1)S(1)}, bf16[2048,256]{1,0:T(8,128)(2,1)}, u32[]{:S(2)}) copy-start(bf16[2048,256]{1,0:T(8,128)(2,1)} %param.8) | copy-start | bytes 3145732
Sparse Core Ops, SparseCore 0:
  10.0 140.6 all-gather.2
  153.8 55.1 all-gather.4
  237.0 453.0 all-reduce.1
where the time goes:
time: 703 us; the launch traced here: 702 us
  waiting for transfers between devices  505 us (72%)
  blocking collectives  89.4 us (13%)
  matrix products  64.5 us (9%)
  other arithmetic  25.3 us (4%)
  between operations  13.8 us (2%)
    psum x1, waiting for transfers between devices, local(): modal_csd = lax.psum(partial_csd, ('row', 'col'))  453 us
    all_gather x1, blocking collectives, local(): piece_points = lax.all_gather(coords, 'row', axis=1, tiled=True)  69.6 us
    dot_general x4, matrix products, add_block(): jnp.dot(part_shapes, coherence_tile, preferred_element_type=jnp.float32)  56.4 us
    all_gather x1, waiting for transfers between devices, local(): piece_shapes = lax.all_gather(mode_shapes, 'row', axis=1, tiled=True)  50.3 us
    reduce_sum x4, other arithmetic, coherence(): squared = jnp.sum(difference * difference, axis=0)  25.3 us
    all_gather x1, blocking collectives, local(): lax.all_gather(coords, 'col', axis=1, tiled=True)  19.8 us
  transfers between devices with their start and end apart: 3, of which 2 were waited for; matrix products, arithmetic and copies ran while one was open for 12% of the time, Pallas kernels for 0%

commit v1 on v0

--- a/solution.py
+++ b/solution.py
@@ -51,7 +51,7 @@
 
     projection = lax.fori_loop(0, block_count, add_block, zero_block)
     partial_csd = modal_product(row_shapes, projection)
-    modal_csd = lax.psum(partial_csd, ("row", "col"))
+    modal_csd = lax.psum(lax.psum(partial_csd, "row"), "col")
     real_part = response_gain[0]
     imag_part = response_gain[1]
     weighted = (

time: 703 us -> 661 us (0.940)
  the two profiles are of different devices: /device:TPU:4 before, /device:TPU:1 now
where the time goes in v1:
time: 661 us
  waiting for transfers between devices  460 us (70%)
  blocking collectives  95.3 us (14%)
  matrix products  64.1 us (10%)
  other arithmetic  25.3 us (4%)
  between operations  13.8 us (2%)
    psum x2, waiting for transfers between devices, local(): modal_csd = lax.psum(lax.psum(partial_csd, 'row'), 'col')  432 us
    all_gather x1, blocking collectives, local(): piece_points = lax.all_gather(coords, 'row', axis=1, tiled=True)  57.3 us
    dot_general x4, matrix products, add_block(): jnp.dot(part_shapes, coherence_tile, preferred_element_type=jnp.float32)  56.4 us
    all_gather x1, blocking collectives, local(): lax.all_gather(coords, 'col', axis=1, tiled=True)  37.9 us
    all_gather x1, waiting for transfers between devices, local(): piece_shapes = lax.all_gather(mode_shapes, 'row', axis=1, tiled=True)  25.8 us
    reduce_sum x4, other arithmetic, coherence(): squared = jnp.sum(difference * difference, axis=0)  25.3 us
  transfers between devices with their start and end apart: 4, of which 3 were waited for; matrix products, arithmetic and copies ran while one was open for 12% of the time, Pallas kernels for 0%

profile of v1, /device:TPU:1, one launch (start us, length us, event | category | flops | bytes accessed | tf_op | source)
XLA Modules:
  0.0 661.0 jit_solution(8721217293561054715)
XLA Ops:
  7.2 0.0 all-gather.3.cloned.1.call-start
  7.2 0.7 all-gather.3.cloned.1.call-update
  7.9 0.0 all-gather.5.cloned.1.call-start
  7.9 0.7 all-gather.5.cloned.1.call-update
  8.6 0.0 all-reduce.3.cloned.1.call-start
  8.7 57.3 %all_gather.13 = s32[3,4096]{1,0:T(4,128)S(1)} all-gather(s32[3,128]{1,0:T(4,128)} %param.6), channel_id=1, replica_groups=mesh['row'=32,'col'=16] {'row'}, dimensions={1}, use_global_device_ids=true | all-gather | bytes 50688 | tf_op jit(solution)/shard_map/all_gather | solution.py:38
  66.0 37.9 %all_gather.14 = s32[3,2048]{1,0:T(4,128)S(1)} all-gather(s32[3,128]{1,0:T(4,128)} %param.6), channel_id=1, replica_groups=mesh['row'=32,'col'=16] {'col'}, dimensions={1}, use_global_device_ids=true | all-gather | bytes 26112 | tf_op jit(solution)/shard_map/all_gather | solution.py:33
  104.0 25.8 %all-gather.3.cloned.1.call-done = bf16[256,4096]{1,0:T(8,128)(2,1)} async-done(((bf16[256,128]{1,0:T(8,128)(2,1)}), bf16[256,4096]{1,0:T(8,128)(2,1)}) %all-gather.3.cloned.1.call-update) | async-done | bytes 2097168 | tf_op jit(solution)/shard_map/all_gather | solution.py:37
  129.8 0.0 copy-start
  129.8 81.9 %while.16 = (s32[]{:T(128)}, f32[256,2048]{1,0:T(8,128)S(1)}, bf16[256,4096]{1,0:T(8,128)(2,1)}, s32[3,4096]{1,0:T(4,128)S(1)}, s32[3,2048]{1,0:T(4,128)S(1)}, /*index=5*/s32[]{:T(128)}, s32[]{:T(128)}, s32[]{:T(128)}, s32[]{:T(128)}) while((s32[]{:T(128)}, f32[256,2048]{1,0:T(8,128)S(1)}, bf16[256,4096]{1,0:T(8,128)(2,1)}, ...), condition=%wide.region_2.3_spmd.clone, body=%wide.region_0.2_spmd.clone.sunk | while | flops 1171259392 | bytes 21557404 | solution.py:52
  129.9 6.3 multiply_reduce_fusion.2
  136.2 14.1 %fusion.60 = f32[256,2048]{1,0:T(8,128)S(1)} fusion(f32[1024,2048]{1,0:T(8,128)} %multiply_reduce_fusion.2, f32[256,2048]{1,0:T(8,128)S(1)} %get-tuple-element.211, pred[]{:T(512)S(6)} %compare.3, bf16[256,4096]{1,0:T(8,128)(2,1)} %get-tuple-element.221, s32[]{:T(128)S(6)} %select_n.137), kind=kOutput, calls=%fused_computation.26.clone.1 | convolution fusion | flops 1148190720 | bytes 13107205 | tf_op jit(solution)/shard_map/while/body/eval_jaxpr/dot_general | solution.py:48
  150.3 6.3 multiply_reduce_fusion.2
  156.7 14.1 %fusion.60 = f32[256,2048]{1,0:T(8,128)S(1)} fusion(f32[1024,2048]{1,0:T(8,128)} %multiply_reduce_fusion.2, f32[256,2048]{1,0:T(8,128)S(1)} %get-tuple-element.211, pred[]{:T(512)S(6)} %compare.3, bf16[256,4096]{1,0:T(8,128)(2,1)} %get-tuple-element.221, s32[]{:T(128)S(6)} %select_n.137), kind=kOutput, calls=%fused_computation.26.clone.1 | convolution fusion | flops 1148190720 | bytes 13107205 | tf_op jit(solution)/shard_map/while/body/eval_jaxpr/dot_general | solution.py:48
  170.8 6.3 multiply_reduce_fusion.2
  177.2 14.1 %fusion.60 = f32[256,2048]{1,0:T(8,128)S(1)} fusion(f32[1024,2048]{1,0:T(8,128)} %multiply_reduce_fusion.2, f32[256,2048]{1,0:T(8,128)S(1)} %get-tuple-element.211, pred[]{:T(512)S(6)} %compare.3, bf16[256,4096]{1,0:T(8,128)(2,1)} %get-tuple-element.221, s32[]{:T(128)S(6)} %select_n.137), kind=kOutput, calls=%fused_computation.26.clone.1 | convolution fusion | flops 1148190720 | bytes 13107205 | tf_op jit(solution)/shard_map/while/body/eval_jaxpr/dot_general | solution.py:48
  191.3 6.3 multiply_reduce_fusion.2
  197.6 14.1 %fusion.60 = f32[256,2048]{1,0:T(8,128)S(1)} fusion(f32[1024,2048]{1,0:T(8,128)} %multiply_reduce_fusion.2, f32[256,2048]{1,0:T(8,128)S(1)} %get-tuple-element.211, pred[]{:T(512)S(6)} %compare.3, bf16[256,4096]{1,0:T(8,128)(2,1)} %get-tuple-element.221, s32[]{:T(128)S(6)} %select_n.137), kind=kOutput, calls=%fused_computation.26.clone.1 | convolution fusion | flops 1148190720 | bytes 13107205 | tf_op jit(solution)/shard_map/while/body/eval_jaxpr/dot_general | solution.py:48
  211.8 0.0 copy-start.1
  211.8 0.0 all-gather.5.cloned.1.call-done
  211.8 1.7 fusion.37
  213.5 2.4 fusion.35
  215.9 0.0 all-reduce.3.cloned.1.call-update
  215.9 0.0 all-reduce.5.cloned.1.call-start
  216.0 258.1 %all-reduce.3.cloned.1.call-done = f32[256,256]{0,1:T(8,128)} async-done(((f32[256,256]{0,1:T(8,128)}), f32[256,256]{0,1:T(8,128)}) %all-reduce.3.cloned.1.call-update) | async-done | bytes 262160 | tf_op jit(solution)/shard_map/psum | solution.py:54
  474.1 0.0 all-reduce.5.cloned.1.call-update
  474.1 0.0 copy-done
  474.1 0.6 copy.8
  474.8 0.0 copy-done.1
  474.8 174.3 %all-reduce.5.cloned.1.call-done = f32[256,256]{0,1:T(8,128)} async-done(((f32[256,256]{0,1:T(8,128)}), f32[256,256]{0,1:T(8,128)}) %all-reduce.5.cloned.1.call-update) | async-done | bytes 262160 | tf_op jit(solution)/shard_map/psum | solution.py:54
  649.1 1.8 copy.9
  650.9 1.4 fusion.40
  652.4 2.1 fusion.34
  (6 shorter events, 0.0 us)
Async XLA Ops:
  7.2 122.7 %all-gather.3.cloned.1.call-start = ((), (), s32[]{:S(2)}) async-start(), calls=%async_computation | async-start | bytes 2162688 | tf_op jit(solution)/shard_map/all_gather | solution.py:37
  7.9 203.9 %all-gather.5.cloned.1.call-start = ((), (), s32[]{:S(2)}) async-start(), calls=%async_computation.1 | async-start | bytes 1114112 | tf_op jit(solution)/shard_map/all_gather | solution.py:32
  8.6 465.5 %all-reduce.3.cloned.1.call-start = ((), (), s32[]{:S(2)}) async-start(), calls=%async_computation.2 | async-start | bytes 524288 | tf_op jit(solution)/shard_map/psum | solution.py:54
  129.8 344.3 %copy-start = (bf16[2048,256]{1,0:T(8,128)(2,1)S(1)}, bf16[2048,256]{1,0:T(8,128)(2,1)}, u32[]{:S(2)}) copy-start(bf16[2048,256]{1,0:T(8,128)(2,1)} %param.8) | copy-start | bytes 3145732
  211.8 263.0 %copy-start.1 = (f32[2,256]{1,0:T(2,128)S(1)}, f32[2,256]{1,0:T(2,128)}, u32[]{:S(2)}) copy-start(f32[2,256]{1,0:T(2,128)} %param.9) | copy-start | bytes 6148
  215.9 433.2 %all-reduce.5.cloned.1.call-start = ((), (), s32[]{:S(2)}) async-start(), calls=%async_computation.3 | async-start | bytes 524288 | tf_op jit(solution)/shard_map/psum | solution.py:54
Sparse Core Ops, SparseCore 0:
  10.0 119.7 all-gather.2
  133.0 78.7 all-gather.4
  216.1 257.9 all-reduce.2
  477.1 171.9 all-reduce.4
